TPU v7x, 32 devices: a whole 2x2x4 slice. The times are simulated.
32 devices in a mesh: gx: 8 (over y, x, core), gy: 4 (over z).
Axes of the slice: x: 2, y: 2, z: 4, core: 2. Of those that a mesh axis runs over, the one named last changes fastest.
Arguments:
- density: bfloat16 [2048, 128, 128], P(('gx', 'gy')), may hold values from -0.00390625 to 0.00390625
- dest: int32 [2048, 2], P(('gx', 'gy')), may hold values from 0 to 31, all different within a row; in each aligned block of 64 rows (0 to 63, 64 to 127, ...) at most 8 rows name the same one
- code: int32 [2048, 2], P(('gx', 'gy')), may hold values from 0 to 143
- basis: bfloat16 [65536, 1536], P(('gx', 'gy')), may hold values from -6 to 6
- descriptors: float32 [10, 65536], P(None, ('gx', 'gy')), may hold values from -6 to 6
- weights: float32 [65536], P(('gx', 'gy')), may hold values from 0.0055242717 to 0.198873782
- w_in: float32 [11, 128], replicated, may hold values from -1.75 to 1.75
- w_hid1: float32 [128, 128], replicated, may hold values from -0.5 to 0.5
- w_hid2: float32 [128, 128], replicated, may hold values from -0.5 to 0.5
- w_out: float32 [128], replicated, may hold values from -0.5 to 0.5
Outputs:
- fock: float32 [2048, 128, 128], P(('gx', 'gy'))
- energy: float32 [], replicated
Inputs may be any that keep to these rules, and one draw needn't show every extreme that they name: `dest`: the two copies of a pair block go to different domains; among the pair blocks of one device at most 8 copies go to one domain.
All inputs are finite; a program needn't handle non-finite values.
Results may differ from a plain program's by a relative error of at most 0.0044.
Values may be sent and summed in bfloat16 or wider, within the bound.
No kernel may reach another device: no remote copies, remote signals or barrier semaphores. Data moves between devices by JAX's collectives and lax.ppermute only.
A program may use at most 128 MiB of HBM per device.

v0:
```python
import math

import jax
import jax.numpy as jnp
from jax import lax
from jax.sharding import PartitionSpec as P

NBF = 128


def network(density_at, descriptors, w_in, w_hid1, w_hid2, w_out):
    features = jnp.concatenate([density_at[None, :], descriptors], axis=0)
    hidden = jnp.tanh(jnp.dot(w_in.T, features, precision=lax.Precision.HIGHEST))
    hidden = jnp.tanh(jnp.dot(w_hid1.T, hidden, precision=lax.Precision.HIGHEST))
    hidden = jnp.tanh(jnp.dot(w_hid2.T, hidden, precision=lax.Precision.HIGHEST))
    logits = jnp.dot(w_out, hidden, precision=lax.Precision.HIGHEST)
    return -jax.nn.softplus(logits)


def slot_sources(dest, domains, capacity):
    flat_dest = dest.reshape(-1)
    order = jnp.arange(flat_dest.shape[0], dtype=jnp.int32)
    earlier = (flat_dest[None, :] == flat_dest[:, None]) & (order[None, :] < order[:, None])
    rank = jnp.sum(earlier.astype(jnp.int32), axis=1)
    slot = flat_dest * capacity + rank
    return jnp.full((domains * capacity,), -1, jnp.int32).at[slot].set(order)


def body(density, dest, code, basis, descriptors, weights, w_in, w_hid1, w_hid2, w_out):
    domains = lax.axis_size(("gx", "gy"))
    owned = density.shape[0]
    copies = dest.shape[1]
    capacity = max(2, 2 * copies * owned // domains)
    block_width = NBF * NBF
    local_blocks = basis.shape[1] // NBF
    local_pairs = local_blocks * local_blocks
    order_size = local_blocks * NBF
    sources = slot_sources(dest, domains, capacity)
    live = sources >= 0
    safe_item = jnp.maximum(sources, 0)
    pair_of_slot = safe_item // copies
    owned_rows = density.reshape(owned, block_width)
    outgoing = jnp.where(
        live[:, None], jnp.take(owned_rows, pair_of_slot, axis=0), jnp.zeros((), jnp.bfloat16)
    )
    out_code = jnp.where(live, code.reshape(-1)[safe_item], -1)
    inbound, in_code = (
        lax.all_to_all(
            outgoing.reshape(domains, capacity, block_width),
            ("gx", "gy"),
            split_axis=0,
            concat_axis=0,
            tiled=True,
        ),
        lax.all_to_all(
            out_code.reshape(domains, capacity),
            ("gx", "gy"),
            split_axis=0,
            concat_axis=0,
            tiled=True,
        ),
    )
    inbound = inbound.reshape(domains * capacity, block_width)
    in_code = in_code.reshape(-1)
    selector = (in_code[None, :] == jnp.arange(local_pairs, dtype=jnp.int32)[:, None]).astype(
        jnp.bfloat16
    )
    summed = jnp.dot(selector, inbound, preferred_element_type=jnp.float32).astype(jnp.bfloat16)
    dense = (
        summed.reshape(local_blocks, local_blocks, NBF, NBF)
        .transpose(0, 2, 1, 3)
        .reshape(order_size, order_size)
    )
    projected = jnp.dot(basis, dense, preferred_element_type=jnp.float32)
    density_at = jnp.sum(projected * basis.astype(jnp.float32), axis=1)

    def energy_fn(values):
        return network(values, descriptors, w_in, w_hid1, w_hid2, w_out)

    energy_at, pullback = jax.vjp(energy_fn, density_at)
    deriv = pullback(jnp.ones_like(energy_at))[0]
    potential = weights * deriv
    scaled = (potential[:, None] * basis.astype(jnp.float32)).astype(jnp.bfloat16)
    fock_mat = lax.dot_general(
        basis, scaled, (((0,), (0,)), ((), ())), preferred_element_type=jnp.float32
    ).astype(jnp.bfloat16)
    fock_blocks = (
        fock_mat.reshape(local_blocks, NBF, local_blocks, NBF)
        .transpose(0, 2, 1, 3)
        .reshape(local_pairs, block_width)
    )
    replies = jnp.where(
        (in_code >= 0)[:, None],
        jnp.take(fock_blocks, jnp.maximum(in_code, 0), axis=0),
        jnp.zeros((), jnp.bfloat16),
    )
    returned = lax.all_to_all(
        replies.reshape(domains, capacity, block_width),
        ("gx", "gy"),
        split_axis=0,
        concat_axis=0,
        tiled=True,
    )
    returned = returned.reshape(domains * capacity, block_width)
    gather_table = (
        (pair_of_slot[None, :] == jnp.arange(owned, dtype=jnp.int32)[:, None]) & live[None, :]
    ).astype(jnp.bfloat16)
    fock = jnp.dot(gather_table, returned, preferred_element_type=jnp.float32).reshape(
        owned, NBF, NBF
    )
    points = basis.shape[0]
    total = lax.psum(jnp.sum(weights * energy_at), ("gx", "gy"))
    energy = total * jnp.float32(1.0 / (math.sqrt(points) * domains))
    return (fock, energy)


def solution(mesh):
    placed = (
        P(("gx", "gy"), None, None),
        P(("gx", "gy"), None),
        P(("gx", "gy"), None),
        P(("gx", "gy"), None),
        P(None, ("gx", "gy")),
        P(("gx", "gy")),
        P(),
        P(),
        P(),
        P(),
    )
    return jax.shard_map(
        body,
        mesh=mesh,
        in_specs=placed,
        out_specs=(P(("gx", "gy"), None, None), P()),
        check_vma=False,
    )
```

profile of v0, /device:TPU:0, one launch (start us, length us, event | category | flops | bytes accessed | tf_op | source)
XLA Modules:
  0.0 563.3 jit_solution(3779091153852710080)
XLA Ops:
  0.6 0.7 broadcast_multiply_fusion
  1.4 0.8 copy.54
  2.1 0.1 copy.53
  2.2 0.1 mul.64
  2.4 0.1 eq.49
  2.5 0.2 convert_reduce_fusion
  2.7 1.0 scatter_custom_fusion
  3.7 0.8 copy.55
  4.5 0.1 reshape.136
  4.6 1.9 gather_fusion
  6.5 0.7 all_to_all.12
  7.2 7.3 %all-to-all-start = ((s32[32,1,8]{2,1,0:T(1,128)}), s32[32,1,8]{2,1,0:T(1,128)S(1)}, u32[]{:S(2)}, u32[]{:S(2)}) async-start(s32[32,1,8]{2,1,0:T(1,128)} %bitcast.3), calls=%async_computation | async-start | bytes 32768 | tf_op jit(solution)/shard_map/all_to_all | solution.py:55
  14.6 0.1 broadcast_in_dim.67
  14.7 3.0 copy.79
  17.7 9.1 %gather_fusion.1 = bf16[256,16384]{1,0:T(8,128)(2,1)} fusion(bf16[64,16384]{1,0:T(8,128)(2,1)S(1)} %bitcast.84, s32[1024]{0:T(1024)S(1)} %pad_clamp_fusion.1), kind=kCustom, calls=%fused_computation.1 | custom fusion | bytes 16778240 | tf_op jit(solution)/shard_map/jit(_take)/gather | solution.py:44
  26.8 7.6 %fusion.4 = bf16[32,8,16384]{2,1,0:T(8,128)(2,1)} fusion(bf16[256,16384]{1,0:T(8,128)(2,1)} %gather_fusion.1, pred[32,8]{1,0:T(8,128)(4,1)S(1)} %broadcast_in_dim.69, pred[32,8]{1,0:T(8,128)(4,1)S(1)} %broadcast_in_dim.67), kind=kLoop, calls=%fused_computation.13 | loop fusion | flops 8388608 | bytes 16777728 | tf_op jit(solution)/shard_map/jit(_where)/select_n | solution.py:43
  34.4 6.5 %all-to-all-start.1 = ((bf16[32,8,16384]{2,1,0:T(8,128)(2,1)}), bf16[32,8,16384]{2,1,0:T(8,128)(2,1)}, u32[]{:S(2)}, u32[]{:S(2)}) async-start(bf16[32,8,16384]{2,1,0:T(8,128)(2,1)} %fusion.4), calls=%async_computation.1 | async-start | bytes 16777216 | tf_op jit(solution)/shard_map/all_to_all | solution.py:48
  40.9 8.7 %copy.62 = bf16[2048,1536]{0,1:T(8,128)(2,1)} copy(bf16[2048,1536]{1,0:T(8,128)(2,1)} %param.13) | data formatting | bytes 12582912 | tf_op args[3]
  49.6 0.5 broadcast.137
  50.1 0.7 reduce.3
  51.1 0.1 reshape.163
  51.2 0.1 copy.58
  51.3 0.1 copy.60
  51.4 170.9 %all-to-all-done.1 = bf16[32,8,16384]{2,1,0:T(8,128)(2,1)} async-done(((bf16[32,8,16384]{2,1,0:T(8,128)(2,1)}), bf16[32,8,16384]{2,1,0:T(8,128)(2,1)}, u32[]{:S(2)}, u32[]{:S(2)}) %all-to-all-start.1) | async-done | bytes 8388640 | tf_op jit(solution)/shard_map/all_to_all | solution.py:48
  222.3 4.8 fusion.11
  227.1 1.4 copy.69
  228.5 6.4 %copy.61 = bf16[12,12,128,128]{3,1,2,0:T(8,128)(2,1)} copy(bf16[12,12,128,128]{3,2,1,0:T(8,128)(2,1)S(1)} %bitcast.88) | data formatting | bytes 9437184 | tf_op jit(solution)/shard_map/reshape | solution.py:70
  235.0 14.7 %fusion = f32[2048]{0:T(1024)S(1)} fusion(bf16[2048,1536]{0,1:T(8,128)(2,1)S(1)} %bitcast.93, bf16[2048,1536]{1,0:T(8,128)(2,1)S(1)} %bitcast.91, bf16[192,8,12,128]{3,2,1,0:T(8,128)(2,1)} %bitcast.94), kind=kOutput, calls=%fused_computation.7 | convolution fusion | flops 9673111552 | bytes 17309696 | tf_op jit(solution)/shard_map/dot_general | solution.py:74
  249.7 1.8 convolution_tanh_fusion.2
  251.5 1.0 convolution_tanh_fusion.1
  252.5 1.0 fusion.10
  253.5 1.0 fusion.36
  254.5 0.6 multiply_reduce_fusion
  255.1 1.1 convolution_multiply_fusion.1
  256.2 1.0 convolution_multiply_fusion
  257.2 1.0 convolution_bitcast_fusion
  258.2 11.5 %fusion.5 = bf16[1536,1536]{0,1:T(8,128)(2,1)} fusion(bf16[2048,1536]{1,0:T(8,128)(2,1)S(1)} %bitcast.91, bf16[2048,1536]{0,1:T(8,128)(2,1)S(1)} %bitcast.93, f32[2048]{0:T(1024)S(1)} %mul.73), kind=kOutput, calls=%fused_computation.15 | convolution fusion | flops 9675472896 | bytes 17309696 | tf_op jit(solution)/shard_map/dot_general | solution.py:84
  269.8 6.7 %copy.63 = bf16[1536,1536]{1,0:T(8,128)(2,1)} copy(bf16[1536,1536]{0,1:T(8,128)(2,1)} %fusion.5) | data formatting | bytes 9437184 | tf_op jit(solution)/shard_map/convert_element_type | solution.py:86
  276.5 9.6 %reshape.142 = bf16[12,128,12,128]{3,2,1,0:T(8,128)(2,1)} reshape(bf16[1536,1536]{1,0:T(8,128)(2,1)} %copy.63) | data formatting | bytes 9437184 | tf_op jit(solution)/shard_map/reshape | solution.py:88
  286.1 4.2 copy.64
  290.3 6.3 %copy.78 = bf16[18,8,128,128]{3,1,2,0:T(8,128)(2,1)} copy(bf16[18,8,128,128]{3,2,1,0:T(8,128)(2,1)S(1)} %bitcast.89) | data formatting | bytes 9437184
  296.6 19.6 %gather_fusion.2 = bf16[256,16384]{1,0:T(8,128)(2,1)} fusion(bf16[144,16384]{1,0:T(8,128)(2,1)} %bitcast.85, s32[1024]{0:T(1024)S(1)} %pad_clamp_fusion), kind=kCustom, calls=%fused_computation.2 | custom fusion | bytes 16778240 | tf_op jit(solution)/shard_map/jit(_take)/gather | solution.py:94
  316.2 7.6 %fusion.2 = bf16[32,8,16384]{2,1,0:T(8,128)(2,1)} fusion(bf16[256,16384]{1,0:T(8,128)(2,1)} %gather_fusion.2, pred[32,8]{1,0:T(8,128)(4,1)S(1)} %copy.60, pred[32,8]{1,0:T(8,128)(4,1)S(1)} %copy.58), kind=kLoop, calls=%fused_computation.10 | loop fusion | flops 8388608 | bytes 16777728 | tf_op jit(solution)/shard_map/jit(_where)/select_n | solution.py:92
  323.8 8.5 %all-to-all-start.2 = ((bf16[32,8,16384]{2,1,0:T(8,128)(2,1)}), bf16[32,8,16384]{2,1,0:T(8,128)(2,1)}, u32[]{:S(2)}, u32[]{:S(2)}) async-start(bf16[32,8,16384]{2,1,0:T(8,128)(2,1)} %fusion.2), calls=%async_computation.2 | async-start | bytes 16777216 | tf_op jit(solution)/shard_map/all_to_all | solution.py:97
  332.2 206.7 %psum.7 = f32[]{:T(128)} all-reduce(f32[]{:T(128)} %get-tuple-element.16), channel_id=1, replica_groups=mesh['gx'=8,'gy'=4] {'gx','gy'}, use_global_device_ids=true, to_apply=%region_4.5 | all-reduce | flops 1 | bytes 8 | tf_op jit(solution)/shard_map/psum | solution.py:112
  539.6 11.9 %copy.66 = bf16[16384,256]{1,0:T(8,128)(2,1)} copy(bf16[16384,256]{0,1:T(8,128)(2,1)} %bitcast.21) | data formatting | bytes 16777216 | tf_op jit(solution)/shard_map/dot_general | solution.py:108
  551.5 6.0 %fusion.28 = f32[64,128,128]{2,0,1:T(8,128)S(1)} fusion(bf16[128,128,256]{2,1,0:T(8,128)(2,1)} %bitcast.86, s32[256]{0:T(256)S(1)} %get-tuple-element.15, pred[256]{0:T(512)(128)(4,1)S(1)} %get-tuple-element.13), kind=kOutput, calls=%fused_computation.48 | convolution fusion | flops 536903680 | bytes 12584192 | tf_op jit(solution)/shard_map/dot_general | solution.py:108
  557.5 4.4 copy.67
  (43 shorter events, 0.5 us)
Async XLA Ops:
  0.6 251.9 %copy-start = (f32[128,128]{1,0:T(8,128)S(1)}, f32[128,128]{1,0:T(8,128)}, u32[]{:S(2)}) copy-start(f32[128,128]{1,0:T(8,128)} %param.18) | copy-start | bytes 196612
  7.2 27.2 %all-to-all-start = ((s32[32,1,8]{2,1,0:T(1,128)}), s32[32,1,8]{2,1,0:T(1,128)S(1)}, u32[]{:S(2)}, u32[]{:S(2)}) async-start(s32[32,1,8]{2,1,0:T(1,128)} %bitcast.3), calls=%async_computation | async-start | bytes 32768 | tf_op jit(solution)/shard_map/all_to_all | solution.py:55
  34.4 187.9 %all-to-all-start.1 = ((bf16[32,8,16384]{2,1,0:T(8,128)(2,1)}), bf16[32,8,16384]{2,1,0:T(8,128)(2,1)}, u32[]{:S(2)}, u32[]{:S(2)}) async-start(bf16[32,8,16384]{2,1,0:T(8,128)(2,1)} %fusion.4), calls=%async_computation.1 | async-start | bytes 16777216 | tf_op jit(solution)/shard_map/all_to_all | solution.py:48
  227.1 7.8 %slice-start = ((s8[6291456]{0:T(1024)(128)(4,1)}), s8[4194304]{0:T(1024)(128)(4,1)S(1)}, s32[]{:S(2)}) async-start(s8[6291456]{0:T(1024)(128)(4,1)} %bitcast.90), calls=%async_computation.3 | async-start | bytes 8388608
  227.1 7.8 %slice-start.2 = ((s8[6291456]{0:T(1024)(128)(4,1)}), s8[4194304]{0:T(1024)(128)(4,1)S(1)}, s32[]{:S(2)}) async-start(s8[6291456]{0:T(1024)(128)(4,1)} %bitcast.92), calls=%async_computation.5 | async-start | bytes 8388608
  228.5 6.4 %slice-start.1 = ((s8[6291456]{0:T(1024)(128)(4,1)}), s8[2097152]{0:T(1024)(128)(4,1)S(1)}, s32[]{:S(2)}) async-start(s8[6291456]{0:T(1024)(128)(4,1)} %bitcast.90), calls=%async_computation.4 | async-start | bytes 4194304
  228.5 6.4 %slice-start.3 = ((s8[6291456]{0:T(1024)(128)(4,1)}), s8[2097152]{0:T(1024)(128)(4,1)S(1)}, s32[]{:S(2)}) async-start(s8[6291456]{0:T(1024)(128)(4,1)} %bitcast.92), calls=%async_computation.6 | async-start | bytes 4194304
  234.9 14.8 %copy-start.3 = (f32[10,2048]{1,0:T(8,128)S(1)}, f32[10,2048]{1,0:T(8,128)}, u32[]{:S(2)}) copy-start(f32[10,2048]{1,0:T(8,128)} %param.14) | copy-start | bytes 245764
  234.9 14.8 %copy-start.4 = (f32[11,128]{1,0:T(8,128)S(1)}, f32[11,128]{1,0:T(8,128)}, u32[]{:S(2)}) copy-start(f32[11,128]{1,0:T(8,128)} %param.16) | copy-start | bytes 16900
  234.9 16.6 %copy-start.2 = (f32[128,128]{1,0:T(8,128)S(1)}, f32[128,128]{1,0:T(8,128)}, u32[]{:S(2)}) copy-start(f32[128,128]{1,0:T(8,128)} %param.17) | copy-start | bytes 196612
  235.0 18.6 %copy-start.6 = (f32[128]{0:T(128)S(1)}, f32[128]{0:T(128)}, u32[]{:S(2)}) copy-start(f32[128]{0:T(128)} %param.19) | copy-start | bytes 1540
  249.7 4.8 copy-start.5
  323.8 215.9 %all-to-all-start.2 = ((bf16[32,8,16384]{2,1,0:T(8,128)(2,1)}), bf16[32,8,16384]{2,1,0:T(8,128)(2,1)}, u32[]{:S(2)}, u32[]{:S(2)}) async-start(bf16[32,8,16384]{2,1,0:T(8,128)(2,1)} %fusion.2), calls=%async_computation.2 | async-start | bytes 16777216 | tf_op jit(solution)/shard_map/all_to_all | solution.py:97
  551.5 10.5 %copy-start.1 = (f32[128,128]{1,0:T(8,128)S(1)}, f32[128,128]{1,0:T(8,128)}, u32[]{:S(2)}) copy-start(f32[128,128]{1,0:T(8,128)} %param.18) | copy-start | bytes 196612
where the time goes:
time: 571 us; the launch traced here: 563 us
  blocking collectives  207 us (36%)
  waiting for transfers between devices  171 us (30%)
  local copies, waits for them, and re-layouts  98.1 us (17%)
  matrix products  44.8 us (8%)
  starting transfers between devices  22.3 us (4%)
  other arithmetic  17.5 us (3%)
    psum x1, blocking collectives, body(): total = lax.psum(jnp.sum(weights * energy_at), ('gx', 'gy'))  207 us
    all_to_all x1, waiting for transfers between devices, body(): lax.all_to_all(outgoing.reshape(domains, capacity, block_width), ('gx', '...  171 us
    unnamed x29, local copies, waits for them, and re-layouts  25.5 us
    gather x1, local copies, waits for them, and re-layouts, body(): jnp.take(fock_blocks, jnp.maximum(in_code, 0), axis=0)  19.6 us
    dot_general x1, matrix products, body(): projected = jnp.dot(basis, dense, preferred_element_type=jnp.float32)  14.7 us
    dot_general x1, local copies, waits for them, and re-layouts, body(): jnp.dot(gather_table, returned, preferred_element_type=jnp.float32)  11.9 us
    dot_general x1, matrix products, body(): lax.dot_general(basis, scaled, (((0,), (0,)), ((), ())), preferred_elemen...  11.5 us
  transfers between devices with their start and end apart: 3, of which 1 were waited for; matrix products, arithmetic and copies ran while one was open for 5% of the time, Pallas kernels for 0%

commit v1 on v0

v1 whole, which is shorter than its diff:
```python
import functools
import math

import jax
import jax.numpy as jnp
from jax import lax
from jax.experimental import pallas as pl
from jax.experimental.pallas import tpu as pltpu
from jax.sharding import PartitionSpec as P

NBF = 128
META = 8
AXES = ("gx", "gy")
HI = lax.Precision.HIGHEST


def any_spec():
    return pl.BlockSpec(memory_space=pl.ANY)


def smem_spec():
    return pl.BlockSpec(memory_space=pltpu.SMEM)


def vmem_spec():
    return pl.BlockSpec(memory_space=pltpu.VMEM)


def block_rows(rank):
    return pl.ds(pl.multiple_of(rank * NBF, NBF), NBF)


def send_kernel(domains, capacity, dest, code, density, out, slots, count, blocks, codes, codes16, load_sem, out_sem, meta_sem):
    copies, owned = dest.shape
    load = pltpu.make_async_copy(density, blocks, load_sem)
    load.start()

    @pl.loop(0, domains)
    def _(d):
        count[d] = 0

    codes[...] = jnp.full(codes.shape, -1.0, jnp.float32)
    lane = lax.broadcasted_iota(jnp.int32, (META, NBF), 1)

    @pl.loop(0, owned)
    def _(p):
        for t in range(copies):
            d = dest[t, p]
            rank = count[d]
            count[d] = rank + 1
            slots[t, p] = d * capacity + rank
            value = code[t, p].astype(jnp.float32)
            codes[d] = jnp.where(lane == rank, value, codes[d])

    codes16[...] = codes[...].astype(jnp.bfloat16)
    meta = pltpu.make_async_copy(codes16, out.at[:, pl.ds(capacity * NBF, META), :], meta_sem)
    meta.start()
    load.wait()

    @pl.loop(0, owned)
    def _(p):
        for t in range(copies):
            slot = slots[t, p]
            d = slot // capacity
            rank = slot - d * capacity
            pltpu.make_async_copy(blocks.at[p], out.at[d, block_rows(rank)], out_sem).start()

    meta.wait()
    part = out.at[pl.ds(0, copies * owned // capacity), pl.ds(0, capacity * NBF), :]
    pltpu.make_async_copy(part, part, out_sem).wait()


def send_blocks(density, dest, code, domains, capacity):
    owned = density.shape[0]
    copies = dest.shape[1]
    return pl.pallas_call(
        functools.partial(send_kernel, domains, capacity),
        out_shape=(
            jax.ShapeDtypeStruct((domains, capacity * NBF + META, NBF), jnp.bfloat16),
            jax.ShapeDtypeStruct((copies, owned), jnp.int32),
        ),
        in_specs=[smem_spec(), smem_spec(), any_spec()],
        out_specs=(any_spec(), smem_spec()),
        scratch_shapes=[
            pltpu.SMEM((domains,), jnp.int32),
            pltpu.VMEM((owned, NBF, NBF), jnp.bfloat16),
            pltpu.VMEM((domains, META, NBF), jnp.float32),
            pltpu.VMEM((domains, META, NBF), jnp.bfloat16),
            pltpu.SemaphoreType.DMA,
            pltpu.SemaphoreType.DMA,
            pltpu.SemaphoreType.DMA,
        ],
        name="send_blocks",
    )(dest.T, code.T, density)


def domain_kernel(
    capacity,
    codes,
    inbound,
    basis,
    basis_t,
    base_in,
    w_row,
    w_hid1,
    w_hid1_t,
    w_hid2,
    w_hid2_t,
    w_out,
    weights,
    reply,
    seen,
    stage,
    acc,
    dense,
    basis_v,
    basis_tv,
    rho,
    hid1,
    hid2,
    blocks,
    meta,
    in_sem,
    basis_sem,
    out_sem,
    meta_sem,
):
    sources = inbound.shape[0]
    slots = sources * capacity
    points, order = basis.shape
    width = order // NBF
    pairs = width * width
    load_t = pltpu.make_async_copy(basis_t, basis_tv, basis_sem.at[0])
    load_n = pltpu.make_async_copy(basis, basis_v, basis_sem.at[1])

    def fetch(source, rank, slot):
        return pltpu.make_async_copy(inbound.at[source, block_rows(rank)], stage.at[slot], in_sem.at[slot])

    @pl.loop(0, sources)
    def _(source):
        for rank in range(capacity):
            slot = source * capacity + rank

            @pl.when(codes[slot] >= 0)
            def _():
                fetch(source, rank, slot).start()

    load_t.start()
    load_n.start()

    @pl.loop(0, pairs)
    def _(c):
        seen[c] = 0

    @pl.loop(0, slots)
    def _(slot):
        c = codes[slot]

        @pl.when(c >= 0)
        def _():
            fetch(0, 0, slot).wait()
            value = stage[slot].astype(jnp.float32)
            before = seen[c]
            seen[c] = 1

            @pl.when(before == 0)
            def _():
                acc[c] = value

            @pl.when(before != 0)
            def _():
                acc[c] = acc[c] + value

    @pl.loop(0, width)
    def _(a):
        rows = block_rows(a)
        for b in range(width):
            there = seen[a * width + b] != 0
            value = jnp.where(there, acc[a * width + b], 0.0)
            dense[rows, b * NBF : (b + 1) * NBF] = value.astype(jnp.bfloat16)

    load_t.wait()
    tile = 256

    @pl.loop(0, points // tile)
    def _(n):
        cols = pl.ds(pl.multiple_of(n * tile, tile), tile)
        part = basis_tv[:, cols]
        projected = jnp.dot(dense[...], part, preferred_element_type=jnp.float32)
        rho[:, cols] = jnp.sum(projected * part.astype(jnp.float32), axis=0, keepdims=True)

    h1 = jnp.tanh(base_in[...] + w_row[...] * rho[...])
    hid1[...] = h1
    h2 = jnp.tanh(jnp.dot(w_hid1_t[...], h1, precision=HI, preferred_element_type=jnp.float32))
    hid2[...] = h2
    h3 = jnp.tanh(jnp.dot(w_hid2_t[...], h2, precision=HI, preferred_element_type=jnp.float32))
    logits = jnp.sum(w_out[...] * h3, axis=0, keepdims=True)
    decay = jnp.exp(-jnp.abs(logits))
    energy_at = -(jnp.maximum(logits, 0.0) + jnp.log1p(decay))
    slope = -jnp.where(logits >= 0, 1.0, decay) / (1.0 + decay)
    g3 = (w_out[...] * slope) * (1.0 - h3 * h3)
    h2 = hid2[...]
    g2 = jnp.dot(w_hid2[...], g3, precision=HI, preferred_element_type=jnp.float32) * (1.0 - h2 * h2)
    h1 = hid1[...]
    g1 = jnp.dot(w_hid1[...], g2, precision=HI, preferred_element_type=jnp.float32) * (1.0 - h1 * h1)
    deriv = jnp.sum(w_row[...] * g1, axis=0, keepdims=True)
    rho[...] = weights[...] * deriv
    total = jnp.sum(weights[...] * energy_at, axis=1, keepdims=True)
    top = total.astype(jnp.bfloat16).astype(jnp.float32)
    rest = total - top
    middle = rest.astype(jnp.bfloat16).astype(jnp.float32)
    low = rest - middle
    lane = lax.broadcasted_iota(jnp.int32, (META, NBF), 1)
    line = jnp.where(lane == 0, top, jnp.where(lane == 1, middle, jnp.where(lane == 2, low, 0.0)))
    meta[...] = line.astype(jnp.bfloat16)

    @pl.loop(0, sources)
    def _(source):
        pltpu.make_async_copy(meta, reply.at[source, pl.ds(capacity * NBF, META)], meta_sem).start()

    load_n.wait()

    @pl.loop(0, points // NBF)
    def _(n):
        rows = block_rows(n)
        line = jnp.broadcast_to(rho[:, rows], (NBF, NBF))
        column = line.T
        for b in range(width):
            cols = slice(b * NBF, (b + 1) * NBF)
            basis_v[rows, cols] = (column * basis_v[rows, cols].astype(jnp.float32)).astype(jnp.bfloat16)

    @pl.loop(0, width // 2)
    def _(n):
        cols = pl.ds(pl.multiple_of(n * 2 * NBF, 2 * NBF), 2 * NBF)
        result = jnp.dot(basis_tv[...], basis_v[:, cols], preferred_element_type=jnp.float32).astype(jnp.bfloat16)
        for a in range(width):
            for half in range(2):
                blocks[a * width + 2 * n + half] = result[a * NBF : (a + 1) * NBF, half * NBF : (half + 1) * NBF]

    def give(source, rank, c):
        return pltpu.make_async_copy(blocks.at[c], reply.at[source, block_rows(rank)], out_sem)

    @pl.loop(0, sources)
    def _(source):
        for rank in range(capacity):
            c = codes[source * capacity + rank]

            @pl.when(c >= 0)
            def _():
                give(source, rank, c).start()

    @pl.loop(0, slots)
    def _(slot):
        @pl.when(codes[slot] >= 0)
        def _():
            give(0, 0, 0).wait()

    whole = reply.at[:, pl.ds(capacity * NBF, META), :]
    pltpu.make_async_copy(whole, whole, meta_sem).wait()


def domain_build(codes, inbound, basis, basis_t, base_in, w_row, w_hid1, w_hid2, w_out, weights, capacity):
    sources = inbound.shape[0]
    points, order = basis.shape
    hid = w_hid1.shape[0]
    pairs = (order // NBF) ** 2
    return pl.pallas_call(
        functools.partial(domain_kernel, capacity),
        out_shape=jax.ShapeDtypeStruct(inbound.shape, jnp.bfloat16),
        in_specs=[smem_spec(), any_spec(), any_spec(), any_spec()] + [vmem_spec()] * 8,
        out_specs=any_spec(),
        scratch_shapes=[
            pltpu.SMEM((pairs,), jnp.int32),
            pltpu.VMEM((sources * capacity, NBF, NBF), jnp.bfloat16),
            pltpu.VMEM((pairs, NBF, NBF), jnp.float32),
            pltpu.VMEM((order, order), jnp.bfloat16),
            pltpu.VMEM((points, order), jnp.bfloat16),
            pltpu.VMEM((order, points), jnp.bfloat16),
            pltpu.VMEM((1, points), jnp.float32),
            pltpu.VMEM((hid, points), jnp.float32),
            pltpu.VMEM((hid, points), jnp.float32),
            pltpu.VMEM((pairs, NBF, NBF), jnp.bfloat16),
            pltpu.VMEM((META, NBF), jnp.bfloat16),
            pltpu.SemaphoreType.DMA((sources * capacity,)),
            pltpu.SemaphoreType.DMA((2,)),
            pltpu.SemaphoreType.DMA,
            pltpu.SemaphoreType.DMA,
        ],
        compiler_params=pltpu.CompilerParams(vmem_limit_bytes=60 << 20),
        name="domain_build",
    )(
        codes, inbound, basis, basis_t, base_in, w_row[:, None], w_hid1, w_hid1.T, w_hid2, w_hid2.T,
        w_out[:, None], weights[None, :],
    )


def collect_kernel(capacity, scale, slots, returned, fock, energy, parts, result, meta, in_sem, out_sem, meta_sem):
    copies, owned = slots.shape
    meta_in = pltpu.make_async_copy(returned.at[:, pl.ds(capacity * NBF, META), :], meta, meta_sem)
    meta_in.start()

    def fetch(source, rank, p, t):
        return pltpu.make_async_copy(returned.at[source, block_rows(rank)], parts.at[p, t], in_sem.at[p])

    @pl.loop(0, owned)
    def _(p):
        for t in range(copies):
            slot = slots[t, p]
            source = slot // capacity
            fetch(source, slot - source * capacity, p, t).start()

    meta_in.wait()
    lane = lax.broadcasted_iota(jnp.int32, meta.shape, 2)
    row = lax.broadcasted_iota(jnp.int32, meta.shape, 1)
    sent = jnp.where((lane < 3) & (row == 0), meta[...].astype(jnp.float32), 0.0)
    per_source = jnp.sum(jnp.sum(sent, axis=0), axis=0, keepdims=True)
    energy[...] = jnp.sum(per_source, axis=1, keepdims=True) * scale

    def give(p):
        return pltpu.make_async_copy(result.at[p], fock.at[p], out_sem)

    @pl.loop(0, owned)
    def _(p):
        pltpu.make_async_copy(parts.at[p], parts.at[p], in_sem.at[p]).wait()
        total = parts[p, 0].astype(jnp.float32)
        for t in range(1, copies):
            total = total + parts[p, t].astype(jnp.float32)
        result[p] = total
        give(p).start()

    pltpu.make_async_copy(result, fock, out_sem).wait()


def collect_blocks(slots, returned, capacity, scale):
    copies, owned = slots.shape
    sources = returned.shape[0]
    return pl.pallas_call(
        functools.partial(collect_kernel, capacity, scale),
        out_shape=(
            jax.ShapeDtypeStruct((owned, NBF, NBF), jnp.float32),
            jax.ShapeDtypeStruct((1, 1), jnp.float32),
        ),
        in_specs=[smem_spec(), any_spec()],
        out_specs=(any_spec(), vmem_spec()),
        scratch_shapes=[
            pltpu.VMEM((owned, copies, NBF, NBF), jnp.bfloat16),
            pltpu.VMEM((owned, NBF, NBF), jnp.float32),
            pltpu.VMEM((sources, META, NBF), jnp.bfloat16),
            pltpu.SemaphoreType.DMA((owned,)),
            pltpu.SemaphoreType.DMA,
            pltpu.SemaphoreType.DMA,
        ],
        name="collect_blocks",
    )(slots, returned)


def body(density, dest, code, basis, descriptors, weights, w_in, w_hid1, w_hid2, w_out):
    domains = lax.axis_size(AXES)
    owned = density.shape[0]
    copies = dest.shape[1]
    capacity = max(2, 2 * copies * owned // domains)
    points = basis.shape[0]
    outgoing, slots = send_blocks(density, dest, code, domains, capacity)
    inbound = lax.all_to_all(outgoing, AXES, split_axis=0, concat_axis=0, tiled=True)
    basis_t = basis.T
    base_in = jnp.dot(w_in[1:].T, descriptors, precision=HI)
    codes = inbound[:, capacity * NBF, :capacity].astype(jnp.int32).reshape(-1)
    replies = domain_build(
        codes, inbound, basis, basis_t, base_in, w_in[0], w_hid1, w_hid2, w_out, weights, capacity
    )
    returned = lax.all_to_all(replies, AXES, split_axis=0, concat_axis=0, tiled=True)
    scale = 1.0 / (math.sqrt(points) * domains)
    fock, energy = collect_blocks(slots, returned, capacity, scale)
    return (fock, energy[0, 0])


def solution(mesh):
    placed = (
        P(AXES, None, None),
        P(AXES, None),
        P(AXES, None),
        P(AXES, None),
        P(None, AXES),
        P(AXES),
        P(),
        P(),
        P(),
        P(),
    )
    return jax.shard_map(
        body,
        mesh=mesh,
        in_specs=placed,
        out_specs=(P(AXES, None, None), P()),
        check_vma=False,
    )
```

time: 571 us -> 443 us (0.78); the launches traced: 563 us -> 442 us
  local copies, waits for them, and re-layouts: 98.1 us -> 12.4 us
  Pallas kernels: 0 us -> 53.7 us
  matrix products: 44.8 us -> 1.99 us
  other arithmetic: 17.5 us -> 0.89 us
  starting transfers between devices: 22.3 us -> 7.46 us
  blocking collectives: 207 us -> 196 us
    psum x1 -> x0, blocking collectives: 207 us -> none  [body(): total = lax.psum(jnp.sum(weights * energy_at), ('gx', 'gy'))]
    all_to_all x0 -> x1, blocking collectives: none -> 196 us  [body(): lax.all_to_all(replies, AXES, split_axis=0, concat_axis=0, tiled=True)]
    pallas_call x0 -> x3, Pallas kernels: none -> 53.7 us  [the longest x1 43.5 us: domain_build(): pl.pallas_call(functools.partial(domain_kernel, capacity), out_shape=jax....]
    dot_general x11 -> x1, matrix products: 44.8 us -> 1.99 us  [body(): base_in = jnp.dot(w_in[1:].T, descriptors, precision=HI)]
    gather x3 -> x0, local copies, waits for them, and re-layouts: 30.5 us -> none  [the longest x1 19.6 us: body(): jnp.take(fock_blocks, jnp.maximum(in_code, 0), axis=0)]
    reshape x4 -> x0, local copies, waits for them, and re-layouts: 16.2 us -> none  [the longest x1 9.62 us: body(): fock_mat.reshape(local_blocks, NBF, local_blocks, NBF).transpose(0, 2, 1, 3)]
    select_n x5 -> x0, other arithmetic: 15.2 us -> none  [the longest x1 7.6 us: body(): jnp.where((in_code >= 0)[:, None], jnp.take(fock_blocks, jnp.maximum(in_c...]
    unnamed x29 -> x13, local copies, waits for them, and re-layouts: 25.5 us -> 10.3 us
  transfers between devices with their start and end apart: 3 -> 1, of which waited for: 1 -> 1; matrix products, arithmetic and copies ran while one was open for 5% -> 3% of each run, Pallas kernels for 0% -> 0%
where the time goes in v1:
time: 443 us; the launch traced here: 442 us
  blocking collectives  196 us (44%)
  waiting for transfers between devices  169 us (38%)
  Pallas kernels  53.7 us (12%)
  local copies, waits for them, and re-layouts  12.4 us (3%)
  starting transfers between devices  7.46 us (2%)
    all_to_all x1, blocking collectives, body(): lax.all_to_all(replies, AXES, split_axis=0, concat_axis=0, tiled=True)  196 us
    all_to_all x1, waiting for transfers between devices, body(): lax.all_to_all(outgoing, AXES, split_axis=0, concat_axis=0, tiled=True)  169 us
    pallas_call x1, Pallas kernels, domain_build(): pl.pallas_call(functools.partial(domain_kernel, capacity), out_shape=jax....  43.5 us
    unnamed x13, local copies, waits for them, and re-layouts  10.3 us
  transfers between devices with their start and end apart: 1, of which 1 were waited for; matrix products, arithmetic and copies ran while one was open for 3% of the time, Pallas kernels for 0%

profile of v1, /device:TPU:0, one launch (start us, length us, event | category | flops | bytes accessed | tf_op | source)
XLA Modules:
  0.0 442.3 jit_solution(2788714500963707609)
XLA Ops:
  0.6 0.0 copy-start
  0.6 5.0 %send_blocks.1 = (bf16[32,1032,128]{2,1,0:T(8,128)(2,1)}, s32[2,64]{1,0:T(2,128)}) custom-call(s32[2,64]{1,0:T(2,128)} %bitcast.15, s32[2,64]{1,0:T(2,128)} %bitcast.16, bf16[64,128,128]{2,1,0:T(8,128)(2,1)} %density.1), custom_call_target="tpu_custom_call" | custom-call | tf_op jit(solution)/shard_map/send_blocks/pallas_call | solution.py:76
  5.7 7.5 %all-to-all-start = ((bf16[32,1032,128]{2,1,0:T(8,128)(2,1)}), bf16[32,1032,128]{2,1,0:T(8,128)(2,1)}, u32[]{:S(2)}, u32[]{:S(2)}) async-start(bf16[32,1032,128]{2,1,0:T(8,128)(2,1)} %get-tuple-element.7), calls=%async_computation | async-start | bytes 16908288 | tf_op jit(solution)/shard_map/all_to_all | solution.py:364
  13.2 0.0 copy-start.3
  13.2 0.0 copy-start.1
  13.2 0.0 copy-start.2
  13.2 0.0 copy-start.4
  13.2 8.8 %copy.17 = bf16[2048,1536]{0,1:T(8,128)(2,1)} copy(bf16[2048,1536]{1,0:T(8,128)(2,1)} %basis.1) | data formatting | bytes 12582912 | tf_op args[3]
  22.0 0.0 copy-done.3
  22.0 0.7 copy.20.w_row
  22.8 0.0 copy-done.1
  22.8 0.7 copy.18
  23.5 0.0 copy-done.2
  23.5 0.7 copy.19
  24.2 0.0 copy-done.4
  24.2 0.7 copy.21.w_out
  24.9 0.0 copy-done
  24.9 2.0 fusion.1.base_in
  26.9 169.0 %all-to-all-done.inbound = bf16[32,1032,128]{2,1,0:T(8,128)(2,1)} async-done(((bf16[32,1032,128]{2,1,0:T(8,128)(2,1)}), bf16[32,1032,128]{2,1,0:T(8,128)(2,1)}, u32[]{:S(2)}, u32[]{:S(2)}) %all-to-all-start) | async-done | bytes 8454176 | tf_op jit(solution)/shard_map/all_to_all | solution.py:364
  195.9 0.9 fusion
  196.8 0.7 reshape.8.codes
  197.5 43.5 %domain_build.1 = bf16[32,1032,128]{2,1,0:T(8,128)(2,1)} custom-call(s32[256]{0:T(256)} %reshape.8.codes, bf16[32,1032,128]{2,1,0:T(8,128)(2,1)} %all-to-all-done.inbound, bf16[2048,1536]{1,0:T(8,128)(2,1)} %basis.1, bf16[1536,2048]{1,0:T(8,128)(2,1)} %bitcast.11, f32[128,2048]{1,0:T(8,128)} %fusion.1.base_in, f32[128,1]{1,0:T(8,128)} %copy.20.w_row, ...), custom_call_target="tpu_custom_call" | custom-call | tf_op jit(solution)/shard_map/domain_build/pallas_call | solution.py:267
  241.0 196.2 %all_to_all.10.returned = bf16[32,1032,128]{2,1,0:T(8,128)(2,1)} all-to-all(bf16[32,1032,128]{2,1,0:T(8,128)(2,1)} %domain_build.1), channel_id=1, replica_groups=mesh['gx'=8,'gy'=4] {'gx','gy'}, dimensions={0} | all-to-all | bytes 16908288 | tf_op jit(solution)/shard_map/all_to_all | solution.py:371
  437.2 5.1 %collect_blocks.1 = (f32[64,128,128]{2,1,0:T(8,128)}, f32[1,1]{1,0:T(1,128)}) custom-call(s32[2,64]{1,0:T(2,128)} %get-tuple-element.6.slots, bf16[32,1032,128]{2,1,0:T(8,128)(2,1)} %all_to_all.10.returned), custom_call_target="tpu_custom_call" | custom-call | tf_op jit(solution)/shard_map/collect_blocks/pallas_call | solution.py:337
  (1 shorter events, 0.0 us)
Async XLA Ops:
  0.6 24.3 %copy-start = (f32[10,2048]{1,0:T(8,128)S(1)}, f32[10,2048]{1,0:T(8,128)}, u32[]{:S(2)}) copy-start(f32[10,2048]{1,0:T(8,128)} %param.14) | copy-start | bytes 245764
  5.7 190.2 %all-to-all-start = ((bf16[32,1032,128]{2,1,0:T(8,128)(2,1)}), bf16[32,1032,128]{2,1,0:T(8,128)(2,1)}, u32[]{:S(2)}, u32[]{:S(2)}) async-start(bf16[32,1032,128]{2,1,0:T(8,128)(2,1)} %get-tuple-element.7), calls=%async_computation | async-start | bytes 16908288 | tf_op jit(solution)/shard_map/all_to_all | solution.py:364
  13.2 8.9 %copy-start.3 = (f32[11,128]{1,0:T(8,128)S(1)}, f32[11,128]{1,0:T(8,128)}, u32[]{:S(2)}) copy-start(f32[11,128]{1,0:T(8,128)} %param.16) | copy-start | bytes 16900
  13.2 9.6 %copy-start.1 = (f32[128,128]{1,0:T(8,128)S(1)}, f32[128,128]{1,0:T(8,128)}, u32[]{:S(2)}) copy-start(f32[128,128]{1,0:T(8,128)} %w_hid1.1) | copy-start | bytes 196612
  13.2 10.3 %copy-start.2 = (f32[128,128]{1,0:T(8,128)S(1)}, f32[128,128]{1,0:T(8,128)}, u32[]{:S(2)}) copy-start(f32[128,128]{1,0:T(8,128)} %w_hid2.1) | copy-start | bytes 196612
  13.2 11.0 %copy-start.4 = (f32[128]{0:T(128)S(1)}, f32[128]{0:T(128)}, u32[]{:S(2)}) copy-start(f32[128]{0:T(128)} %param.19) | copy-start | bytes 1540
